TPU v7x, 32 devices: a whole 2x2x4 slice. The times are simulated.
32 devices in a mesh: row: 8 (over z, x), col: 4 (over y, core).
Axes of the slice: x: 2, y: 2, z: 4, core: 2. Of those that a mesh axis runs over, the one named last changes fastest.
Arguments:
- coeffs: float32 [4096, 4096], P('row', 'col'), may hold values from -6 to 6
- ham_alpha: float32 [4096, 4096], P('row'), may hold values from -1.5 to 7.5, as said below
- ham_beta: float32 [4096, 4096], P('col'), may hold values from -1.5 to 7.5, as said below
Outputs:
- sigma_vec: float32 [4096, 4096], P('row', 'col')
Inputs may be any that keep to these rules, and one draw needn't show every extreme that they name: `ham_alpha`: symmetric. `ham_beta`: symmetric.
All inputs are finite; a program needn't handle non-finite values.
Results may differ from a plain program's by a relative error of at most 0.00005.
Values sent between devices are 32-bit elements; how exact they have to be, the bound alone decides.
A program may use at most 128 MiB of HBM per device.

v0:
```python
import functools

import jax
import jax.numpy as jnp
from jax import lax
from jax.experimental import pallas as pl
from jax.experimental.pallas import tpu as pltpu
from jax.sharding import PartitionSpec as P

PAIR = 2
MESH = pl.DeviceIdType.MESH


def flip(index, key):
    bit = 1
    while bit <= key:
        if key & bit:
            index = index + bit - 2 * bit * ((index // bit) % 2)
        bit *= 2
    return index


def split(value):
    high = value.astype(jnp.bfloat16)
    return high, (value - high.astype(jnp.float32)).astype(jnp.bfloat16)


def product(lhs, rhs, rhs_dim):
    lhs_high, lhs_low = split(lhs)
    rhs_high, rhs_low = split(rhs)

    def one(a, b):
        return lax.dot_general(
            a, b, (((1,), (rhs_dim,)), ((), ())), preferred_element_type=jnp.float32
        )

    return one(lhs_high, rhs_high) + (one(lhs_high, rhs_low) + one(lhs_low, rhs_high))


def exchanges(n):
    held, mask, out = [0], n // 2, []
    while mask:
        out += [(mask, key) for key in held]
        held += [key ^ mask for key in held]
        mask //= 2
    return out


def kernel(
    line, cols_n, cw, width,
    coeffs, ha, hb, out,
    ham, beta, co, ag, sums, sums_in, acc, acc_in, turned, back_in,
    load_sem, ag_send, ag_recv, s_send, s_recv, o_send, o_recv,
    x_send, x_recv, p_send, p_recv, c_send, c_recv,
):
    rows, cols = coeffs.shape
    nk = cols // cw - 1
    row, col = lax.axis_index("row"), lax.axis_index("col")
    z, x = row // PAIR, row % PAIR
    partner = z * PAIR + 1 - x
    steps = exchanges(cols_n)
    masks = sorted({mask for mask, _ in steps}, reverse=True)

    def there(to_row, to_col):
        return (to_row, to_col)

    def ham_load(s):
        at = pl.multiple_of((s * PAIR + x) * rows, 128)
        return pltpu.make_async_copy(ha.at[:, pl.ds(at, rows)], ham.at[0, s], load_sem.at[s])

    def beta_load(key):
        at = pl.multiple_of(flip(col, key) * cols, 128)
        return pltpu.make_async_copy(
            hb.at[:, pl.ds(at, cols)], beta.at[key], load_sem.at[line + key]
        )

    beta_load(0).start()
    for s in range(line):
        ham_load(s).start()
    for key in range(1, cols_n):
        beta_load(key).start()

    barrier = pltpu.get_barrier_semaphore()
    has_low, has_high = z > 0, z < line - 1
    pl.semaphore_signal(barrier, inc=1, device_id=there(partner, col), device_id_type=MESH)
    for mask in masks:
        pl.semaphore_signal(
            barrier, inc=1, device_id=there(row, flip(col, mask)), device_id_type=MESH
        )

    @pl.when(has_low)
    def _():
        pl.semaphore_signal(barrier, inc=1, device_id=there(row - PAIR, col), device_id_type=MESH)

    @pl.when(has_high)
    def _():
        pl.semaphore_signal(barrier, inc=1, device_id=there(row + PAIR, col), device_id_type=MESH)

    inner = jnp.logical_and(has_low, has_high)

    @pl.when(inner)
    def _():
        pl.semaphore_wait(barrier, 3 + len(masks))

    @pl.when(jnp.logical_not(inner))
    def _():
        pl.semaphore_wait(barrier, 2 + len(masks))

    def remote(src, dst, send, recv, to):
        return pltpu.make_async_remote_copy(
            src_ref=src, dst_ref=dst, send_sem=send, recv_sem=recv,
            device_id=to, device_id_type=MESH,
        )

    def slot(index):
        first = index * width
        at = pl.multiple_of(first % rows, 128)
        return ham.at[1, first // rows, :, pl.ds(at, width)]

    def piece_copy():
        first = col * width
        at = pl.multiple_of((first // rows * PAIR + 1 - x) * rows + first % rows, 128)
        return remote(
            ha.at[:, pl.ds(at, width)], slot(col), x_send.at[0], x_recv.at[0], there(partner, col)
        )

    def back_copy():
        return remote(
            coeffs.at[:, pl.ds(nk * cw, cw)], back_in, x_send.at[1], x_recv.at[1],
            there(partner, col),
        )

    def other_copy(k):
        return remote(acc.at[1, k], acc_in.at[k], o_send.at[k], o_recv.at[k], there(partner, col))

    def ag_copy(d, t, k):
        src = coeffs.at[:, pl.ds(pl.multiple_of(k * cw, 128), cw)] if t == 1 else ag.at[d, t - 2, k]
        to = there(row + PAIR if d == 0 else row - PAIR, col)
        return remote(src, ag.at[d, t - 1, k], ag_send.at[d, t - 1, k], ag_recv.at[d, t - 1, k], to)

    def ag_sends(d, t):
        if d == 0:
            return jnp.logical_and(has_high, z >= t - 1)
        return jnp.logical_and(has_low, z <= line - t)

    def ag_gets(d, t):
        return z >= t if d == 0 else z <= line - 1 - t

    def s_copy(d, m):
        to = there(row + PAIR if d == 0 else row - PAIR, col)
        return remote(sums.at[d, m - 1], sums_in.at[d, m - 1], s_send.at[d, m - 1], s_recv.at[d, m - 1], to)

    def s_sends(d, m):
        return z <= line - 1 - m if d == 0 else z >= m

    def s_gets(d, m):
        if d == 0:
            return jnp.logical_and(z >= 1, z - 1 <= line - 1 - m)
        return jnp.logical_and(z <= line - 2, z + 1 >= m)

    def p_copy(i):
        mask, key = steps[i]
        place = slot(flip(col, key))
        return remote(place, place, p_send.at[i], p_recv.at[i], there(row, flip(col, mask)))

    def p_got(i):
        mask, key = steps[i]
        place = slot(flip(col, key ^ mask))
        return remote(place, place, p_send.at[i], p_recv.at[i], there(row, flip(col, mask)))

    half = rows // 2

    def c_copy(i, h):
        mask, key = steps[i]
        part = pl.ds(h * half, half)
        src = coeffs.at[part] if key == 0 else co.at[key - 1, part]
        return remote(
            src, co.at[(key ^ mask) - 1, part], c_send.at[i, h], c_recv.at[i, h],
            there(row, flip(col, mask)),
        )

    piece_copy().start()
    for d in range(2):
        @pl.when(ag_sends(d, 1))
        def _(d=d):
            for k in range(nk):
                ag_copy(d, 1, k).start()
    c_copy(0, 0).start()
    back_copy().start()

    tile = min(256, cols)

    def beta_tile(key_ref, beta_ref, n, add):
        at = pl.ds(pl.multiple_of(n * tile, 128), tile)
        value = product(key_ref[...], beta_ref[at, :], 1)
        out[:, at] = out[:, at] + value if add else value

    beta_load(0).wait()

    @pl.loop(0, cols // tile)
    def _(n):
        beta_tile(coeffs, beta.at[0], n, False)

    turned[0] = coeffs[:, nk * cw:].T
    for s in range(line):
        ham_load(s).wait()
    for key in range(1, cols_n):
        beta_load(key).wait()

    piece_copy().wait_recv()
    p_copy(0).start()
    c_copy(0, 1).start()

    def pass_on(t, ks):
        for k in ks:
            for d in range(2):
                @pl.when(ag_gets(d, t))
                def _(d=d, k=k):
                    ag_copy(d, t, k).wait_recv()

                if t + 1 < line:
                    @pl.when(ag_sends(d, t + 1))
                    def _(d=d, k=k):
                        ag_copy(d, t + 1, k).start()

    pass_on(1, range(nk))

    for mask in masks:
        group = [i for i, step in enumerate(steps) if step[0] == mask]
        for i in group:
            if i:
                p_copy(i).start()
        for i in group:
            p_got(i).wait_recv()
    back_copy().wait_recv()
    turned[1] = back_in[...].T

    def term(s):
        def body(m, total):
            return total + product(turned[m], ham[m, s], 0)

        return lax.fori_loop(0, PAIR, body, jnp.zeros((cw, rows), jnp.float32))

    def send_sums(m):
        for d in range(2):
            @pl.when(s_sends(d, m))
            def _(d=d):
                sums[d, m - 1] = term(z + m if d == 0 else z - m)

            if m + 1 < line:
                @pl.when(s_gets(d, m + 1))
                def _(d=d):
                    s_copy(d, m + 1).wait_recv()

                @pl.when(jnp.logical_and(s_gets(d, m + 1), s_sends(d, m)))
                def _(d=d):
                    sums[d, m - 1] = sums[d, m - 1] + sums_in[d, m]

            @pl.when(s_sends(d, m))
            def _(d=d):
                s_copy(d, m).start()

    def add_products(d, t, k):
        s = z - t if d == 0 else z + t

        @pl.loop(0, PAIR)
        def _(m):
            acc[m, k] = acc[m, k] + product(ham[m, s], ag[d, t - 1, k], 0)

    def add_step(t):
        for d in range(2):
            @pl.when(ag_gets(d, t))
            def _(d=d):
                @pl.loop(0, nk)
                def _(k):
                    add_products(d, t, k)

    early = line > 3
    if early:
        pass_on(2, range(min(1, nk)))
    send_sums(line - 1)
    if early:
        pass_on(2, range(1, nk - 1))

    @pl.loop(0, nk)
    def _(k):
        own = coeffs.at[:, pl.ds(pl.multiple_of(k * cw, 128), cw)]

        @pl.loop(0, PAIR)
        def _(m):
            acc[m, k] = product(ham[m, z], own[...], 0)

    def coeffs_step(mask):
        group = [i for i, step in enumerate(steps) if step[0] == mask]
        for i in group:
            if i:
                for h in range(2):
                    c_copy(i, h).start()
        for i in group:
            for h in range(2):
                c_copy(i, h).wait_recv()

    if early:
        pass_on(2, range(max(1, nk - 1), nk))
    for t in range(2, line):
        if 2 < t < line - 1:
            pass_on(t, range(nk))
        if t < line - 1:
            send_sums(line - t)
        if t == 2:
            coeffs_step(masks[0])
            if len(masks) > 1:
                for i, step in enumerate(steps):
                    if step[0] == masks[1]:
                        for h in range(2):
                            c_copy(i, h).start()
        add_step(t - 1)

    def coeffs_rest():
        for j, mask in enumerate(masks):
            group = [i for i, step in enumerate(steps) if step[0] == mask]
            if j >= 2:
                for i in group:
                    for h in range(2):
                        c_copy(i, h).start()
            if j >= 1:
                for i in group:
                    for h in range(2):
                        c_copy(i, h).wait_recv()

    def add_beta(key):
        @pl.loop(0, cols // tile)
        def _(n):
            beta_tile(co.at[key - 1], beta.at[key], n, True)

    t = line - 1
    for k in range(nk):
        for d in range(2):
            @pl.when(ag_gets(d, t))
            def _(d=d, k=k):
                ag_copy(d, t, k).wait_recv()
                add_products(d, t, k)

        other_copy(k).start()
        if k == 0:
            send_sums(1)
            coeffs_rest()
        if k + 1 < cols_n:
            add_beta(k + 1)

    @pl.loop(nk + 1, cols_n)
    def _(key):
        add_beta(key)

    tail = term(z)
    for d in range(2):
        @pl.when(s_gets(d, 1))
        def _(d=d):
            s_copy(d, 1).wait_recv()
    sums[0, line - 1] = tail
    for d in range(2):
        @pl.when(s_gets(d, 1))
        def _(d=d):
            sums[0, line - 1] = sums[0, line - 1] + sums_in[d, 0]
    out[:, nk * cw:] = out[:, nk * cw:] + sums[0, line - 1].T

    @pl.loop(0, nk)
    def _(k):
        at = pl.ds(pl.multiple_of(k * cw, 128), cw)
        other_copy(k).wait_recv()
        out[:, at] = out[:, at] + (acc[0, k] + acc_in[k])

    piece_copy().wait_send()
    back_copy().wait_send()
    for i in range(len(steps)):
        p_copy(i).wait_send()
        for h in range(2):
            c_copy(i, h).wait_send()
    for d in range(2):
        for m in range(1, line):
            @pl.when(ag_sends(d, m))
            def _(d=d, m=m):
                for k in range(nk):
                    ag_copy(d, m, k).wait_send()

            @pl.when(s_sends(d, m))
            def _(d=d, m=m):
                s_copy(d, m).wait_send()

    @pl.loop(0, nk)
    def _(k):
        other_copy(k).wait_send()


def solution(mesh):
    line, cols_n = mesh.shape["row"] // PAIR, mesh.shape["col"]
    n_steps = len(exchanges(cols_n))

    def local(coeffs, ham_alpha, ham_beta):
        rows, cols = coeffs.shape
        cw = min(256, cols // 2)
        nk = cols // cw - 1
        width = line * rows // cols_n
        f32, dma = jnp.float32, pltpu.SemaphoreType.DMA
        any_spec = pl.BlockSpec(memory_space=pl.ANY)
        vmem_spec = pl.BlockSpec(memory_space=pltpu.VMEM)
        return pl.pallas_call(
            functools.partial(kernel, line, cols_n, cw, width),
            out_shape=jax.ShapeDtypeStruct((rows, cols), f32),
            in_specs=[vmem_spec, any_spec, any_spec],
            out_specs=vmem_spec,
            scratch_shapes=[
                pltpu.VMEM((PAIR, line, rows, rows), f32),
                pltpu.VMEM((cols_n, cols, cols), f32),
                pltpu.VMEM((cols_n - 1, rows, cols), f32),
                pltpu.VMEM((2, line - 1, nk, rows, cw), f32),
                pltpu.VMEM((2, line, cw, rows), f32),
                pltpu.VMEM((2, line - 1, cw, rows), f32),
                pltpu.VMEM((PAIR, nk, rows, cw), f32),
                pltpu.VMEM((nk, rows, cw), f32),
                pltpu.VMEM((PAIR, cw, rows), f32),
                pltpu.VMEM((rows, cw), f32),
                dma((line + cols_n,)),
                dma((2, line - 1, nk)),
                dma((2, line - 1, nk)),
                dma((2, line - 1)),
                dma((2, line - 1)),
                dma((nk,)),
                dma((nk,)),
                dma((2,)),
                dma((2,)),
                dma((n_steps,)),
                dma((n_steps,)),
                dma((n_steps, 2)),
                dma((n_steps, 2)),
            ],
            compiler_params=pltpu.CompilerParams(
                collective_id=0, has_side_effects=True, vmem_limit_bytes=67043328
            ),
        )(coeffs, ham_alpha, ham_beta)

    in_specs = (P("row", "col"), P("row", None), P("col", None))
    return jax.shard_map(
        local, mesh=mesh, in_specs=in_specs, out_specs=P("row", "col"), check_vma=False
    )
```

profile of v0, /device:TPU:0, one launch (start us, length us, event | category | flops | bytes accessed | tf_op | source)
XLA Modules:
  0.0 126.9 jit_solution(8796416019306074143)
XLA Ops:
  0.0 123.7 %shard_map.37 = f32[512,1024]{1,0:T(8,128)} custom-call(f32[512,1024]{1,0:T(8,128)} %coeffs.1, f32[512,4096]{1,0:T(8,128)} %ha.1, f32[1024,4096]{1,0:T(8,128)} %hb.1), custom_call_target="tpu_custom_call" | custom-call | tf_op jit(solution)/shard_map/pallas_call | solution.py:407
  123.7 3.2 %copy.5 = f32[512,1024]{1,0:T(8,128)} copy(f32[512,1024]{1,0:T(8,128)} %shard_map.37) | data formatting | bytes 4194304
where the time goes:
time: 127 us
  Pallas kernels  124 us (98%)
  local copies, waits for them, and re-layouts  3.16 us (2%)
    pallas_call x1, Pallas kernels, local(): pl.pallas_call(functools.partial(kernel, line, cols_n, cw, width), out_sh...  124 us
    unnamed x1, local copies, waits for them, and re-layouts  3.16 us

commit v1 on v0

v1 whole, which is shorter than its diff:
```python
import functools

import jax
import jax.numpy as jnp
from jax import lax
from jax.experimental import pallas as pl
from jax.experimental.pallas import tpu as pltpu
from jax.sharding import PartitionSpec as P

PAIR = 2
LANES = 128
MESH = pl.DeviceIdType.MESH


def flip(index, key):
    bit = 1
    while bit <= key:
        if key & bit:
            index = index + bit - 2 * bit * ((index // bit) % 2)
        bit *= 2
    return index


def split(value):
    high = value.astype(jnp.bfloat16)
    return high, (value - high.astype(jnp.float32)).astype(jnp.bfloat16)


def product(lhs, rhs, lhs_dim, rhs_dim):
    lhs_high, lhs_low = split(lhs)
    rhs_high, rhs_low = split(rhs)

    def one(a, b):
        return lax.dot_general(
            a, b, (((lhs_dim,), (rhs_dim,)), ((), ())), preferred_element_type=jnp.float32
        )

    return one(lhs_high, rhs_high) + (one(lhs_high, rhs_low) + one(lhs_low, rhs_high))


def exchanges(n):
    held, mask, out = [0], n // 2, []
    while mask:
        out += [(mask, key) for key in held]
        held += [key ^ mask for key in held]
        mask //= 2
    return out


def kernel(
    line, cols_n, cw,
    coeffs, ha, hb, result,
    own, out, ham, beta, co, ag, rs, acc, acc_in, pair,
    l_sem, h_sem, b_sem, out_sem, a_send, a_recv, r_send, r_recv,
    x_send, x_recv, k_send, k_recv, o_send, o_recv, p_send, p_recv, c_send, c_recv,
):
    rows, cols = coeffs.shape
    nc = cols // 2 // cw
    units = cols // LANES
    prow = rows // cols_n
    tile = min(256, cols)
    row, col = lax.axis_index("row"), lax.axis_index("col")
    z, x = row // PAIR, row % PAIR
    partner = z * PAIR + 1 - x
    steps = exchanges(cols_n)
    masks = sorted({mask for mask, _ in steps}, reverse=True)
    groups = [[i for i, step in enumerate(steps) if step[0] == mask] for mask in masks]
    near = steps.index((1, 0))

    def lanes(c, width=cw):
        return pl.ds(pl.multiple_of(c * width, LANES), width)

    def sum_lanes(c):
        return pl.ds(pl.multiple_of((nc + c) * cw, LANES), cw)

    def place(f):
        return z + f * (line - 1 - 2 * z)

    def turn(index, f):
        return index + f * (line - 1 - 2 * index)

    side = (2 * z) // line
    low_z = z + side * (line - 1 - 2 * z)

    def slot(i):
        late = (i + low_z + 1) // line
        s = (1 - late) * (line - 1 - i) + late * (i - (line - 1 - low_z))
        return s + side * (line - 1 - 2 * s)

    def remote(src, dst, send, recv, to):
        return pltpu.make_async_remote_copy(
            src_ref=src, dst_ref=dst, send_sem=send, recv_sem=recv,
            device_id=to, device_id_type=MESH,
        )

    def own_load():
        return pltpu.make_async_copy(coeffs, own, l_sem.at[0])

    def pair_load():
        return pltpu.make_async_copy(
            coeffs.at[:, pl.ds(nc * cw, nc * cw)], pair.at[0], l_sem.at[1]
        )

    def ham_load(s):
        at = pl.multiple_of((s * PAIR + x) * rows, LANES)
        return pltpu.make_async_copy(ha.at[:, pl.ds(at, rows)], ham.at[0, s], h_sem.at[s])

    def beta_load(key):
        at = pl.multiple_of(flip(col, key) * cols, LANES)
        return pltpu.make_async_copy(hb.at[:, pl.ds(at, cols)], beta.at[key], b_sem.at[key])

    own_load().start()
    beta_load(0).start()
    for s in range(line):
        ham_load(s).start()
    pair_load().start()
    for key in range(1, cols_n):
        beta_load(key).start()

    barrier = pltpu.get_barrier_semaphore()
    has_low, has_high = z > 0, z < line - 1

    def greet(to):
        pl.semaphore_signal(barrier, inc=1, device_id=to, device_id_type=MESH)

    greet((partner, col))
    for mask in masks:
        greet((row, flip(col, mask)))

    @pl.when(has_low)
    def _():
        greet((row - PAIR, col))

    @pl.when(has_high)
    def _():
        greet((row + PAIR, col))

    inner = jnp.logical_and(has_low, has_high)

    @pl.when(inner)
    def _():
        pl.semaphore_wait(barrier, 3 + len(masks))

    @pl.when(jnp.logical_not(inner))
    def _():
        pl.semaphore_wait(barrier, 2 + len(masks))

    def onward(f):
        return (row + PAIR - 2 * PAIR * f, col)

    def gather_copy(f, j, c):
        src = coeffs.at[:, lanes(c)] if isinstance(j, int) and j == 0 else ag.at[f, j - 1, :, lanes(c)]
        return remote(
            src, ag.at[f, j, :, lanes(c)], a_send.at[f, j, c], a_recv.at[f, j, c], onward(f)
        )

    def sum_copy(f, j, c):
        return remote(
            rs.at[f, j - 1, :, lanes(c)], rs.at[f, j, :, lanes(c)],
            r_send.at[f, j, c], r_recv.at[f, j, c], onward(f),
        )

    def goes_on(f):
        return place(f) < line - 1

    def piece(i, index):
        return ham.at[1, slot(i), pl.ds(pl.multiple_of(index * prow, 8), prow)]

    def piece_copy(i):
        at = pl.multiple_of((slot(i) * PAIR + 1 - x) * rows, LANES)
        src = ha.at[pl.ds(pl.multiple_of(col * prow, 8), prow), pl.ds(at, rows)]
        return remote(src, piece(i, col), x_send.at[i], x_recv.at[i], (partner, col))

    def pair_copy(c):
        return remote(
            coeffs.at[:, sum_lanes(c)], pair.at[1, :, lanes(c)],
            k_send.at[c], k_recv.at[c], (partner, col),
        )

    def other_copy(c):
        return remote(
            acc.at[1, :, lanes(c)], acc_in.at[:, lanes(c)], o_send.at[c], o_recv.at[c],
            (partner, col),
        )

    def p_copy(n, i):
        mask, key = steps[n]
        part = piece(i, flip(col, key))
        return remote(part, part, p_send.at[n, i], p_recv.at[n, i], (row, flip(col, mask)))

    def p_got(n, i):
        mask, key = steps[n]
        part = piece(i, flip(col, key ^ mask))
        return remote(part, part, p_send.at[n, i], p_recv.at[n, i], (row, flip(col, mask)))

    def c_copy(n, u):
        mask, key = steps[n]
        at = lanes(u, LANES)
        src = coeffs.at[:, at] if key == 0 else co.at[key - 1, :, at]
        return remote(
            src, co.at[(key ^ mask) - 1, :, at], c_send.at[n, u], c_recv.at[n, u],
            (row, flip(col, mask)),
        )

    @pl.when(has_high)
    def _():
        for c in range(nc):
            gather_copy(0, 0, c).start()

    @pl.when(has_low)
    def _():
        for c in range(nc):
            gather_copy(1, 0, c).start()

    piece_copy(0).start()
    c_copy(groups[0][0], 0).start()
    for c in range(nc):
        pair_copy(c).start()
    for i in range(1, line):
        piece_copy(i).start()
    for group in groups[1:]:
        for u in range(units):
            c_copy(group[0], u).start()

    def pass_piece(i):
        piece_copy(i).wait_recv()
        for group in groups:
            p_copy(group[0], i).start()

    def have_piece(i):
        for g, group in enumerate(groups):
            if g:
                for n in group[1:]:
                    p_copy(n, i).start()
            for n in group:
                p_got(n, i).wait_recv()

    def have_units(first, last):
        for g, group in enumerate(groups):
            if g:
                for u in range(first, last):
                    for n in group[1:]:
                        c_copy(n, u).start()
            for u in range(first, last):
                for n in group:
                    if n != near:
                        c_copy(n, u).wait_recv()

    def add_beta(key, add, k_at=0, k_width=cols):
        depth = pl.ds(k_at, k_width)
        lhs = own if key == 0 else co.at[key - 1]

        @pl.loop(0, cols // tile)
        def _(n):
            at = lanes(n, tile)
            value = product(lhs[:, depth], beta[key, at, depth], 1, 1)
            out[:, at] = out[:, at] + value if add else value

    def term(d, c):
        def one(m):
            return product(ham[m, d], pair[m, :, lanes(c)], 0, 0)

        return one(0) + one(1)

    def add_gathered(m, s, f, b, c):
        at = lanes(c)
        acc[m, :, at] = acc[m, :, at] + product(ham[m, s], ag[f, b, :, at], 1, 0)

    own_load().wait()
    beta_load(0).wait()
    add_beta(0, False)
    pass_piece(0)
    for u in range(1, units // 2 + 1):
        c_copy(groups[0][0], u).start()

    for s in range(line):
        ham_load(s).wait()
    pair_load().wait()

    @pl.loop(0, nc)
    def _(c):
        acc[0, :, lanes(c)] = product(ham[0, z], own[:, lanes(c)], 1, 0)

    for key in range(1, cols_n):
        beta_load(key).wait()
    for u in range(units):
        c_copy(near, u).wait_recv()
    add_beta(1, True)
    have_piece(0)

    def second_products(c):
        at = lanes(c)
        acc[1, :, at] = product(ham[1, z], own[:, at], 1, 0)

        @pl.loop(0, 2)
        def _(f):
            for b in range(2):
                @pl.when(b < place(f))
                def _(b=b):
                    add_gathered(1, turn(place(f) - 1 - b, f), f, b, c)

    for j in range(1, line):
        if j == 2:
            pass_piece(1)
            have_units(0, units // 2)
            for key in range(2, cols_n):
                add_beta(key, True, 0, cols // 2)
            have_piece(1)

        @pl.loop(0, nc)
        def _(c, j=j):
            if j == 2:
                @pl.when(c + 2 < line)
                def _():
                    pass_piece(c + 2)

            if j == 1:
                pair_copy(c).wait_recv()

            @pl.loop(0, 2)
            def _(f):
                at = place(f)

                @pl.when(at >= j)
                def _():
                    gather_copy(f, j - 1, c).wait_recv()

                    if j < line - 1:
                        @pl.when(goes_on(f))
                        def _():
                            gather_copy(f, j, c).start()

                @pl.when(jnp.logical_and(at < j, goes_on(f)))
                def _():
                    value = term(turn(line + at - j, f), c)
                    if j == 1:
                        rs[f, j - 1, :, lanes(c)] = value
                    else:
                        @pl.when(at > 0)
                        def _():
                            sum_copy(f, j - 1, c).wait_recv()
                            rs[f, j - 1, :, lanes(c)] = rs[f, j - 1, :, lanes(c)] + value

                        @pl.when(at == 0)
                        def _():
                            rs[f, j - 1, :, lanes(c)] = value

                    sum_copy(f, j, c).start()

            if j == 3:
                second_products(c)

            @pl.loop(0, 2)
            def _(f):
                at = place(f)

                @pl.when(at >= j)
                def _():
                    @pl.loop(0, 1 if j < 3 else PAIR)
                    def _(m):
                        add_gathered(m, turn(at - j, f), f, j - 1, c)

            if j == line - 1:
                other_copy(c).start()

        if j == 2:
            for i in range(nc + 2, line):
                pass_piece(i)
            for u in range(units // 2 + 1, units):
                c_copy(groups[0][0], u).start()
            for i in range(2, line):
                have_piece(i)

    have_units(units // 2, units)
    for key in range(2, cols_n):
        add_beta(key, True, cols // 2, cols // 2)

    @pl.loop(0, nc)
    def _(c):
        at = sum_lanes(c)
        out[:, at] = out[:, at] + term(z, c)

    def out_copy(at, n):
        return pltpu.make_async_copy(out.at[:, at], result.at[:, at], out_sem.at[n])

    def finish_sums(c):
        at = sum_lanes(c)

        @pl.loop(0, 2)
        def _(f):
            @pl.when(place(f) > 0)
            def _():
                sum_copy(f, line - 1, c).wait_recv()
                out[:, at] = out[:, at] + rs[f, line - 1, :, lanes(c)]

        out_copy(at, nc + c).start()

    def finish_gathered(c):
        at = lanes(c)
        other_copy(c).wait_recv()
        out[:, at] = out[:, at] + (acc[0, :, at] + acc_in[:, at])
        out_copy(at, c).start()

    @pl.loop(0, nc - 1)
    def _(c):
        finish_sums(c)

    @pl.loop(0, nc)
    def _(c):
        finish_gathered(c)

    finish_sums(nc - 1)

    for i in range(line):
        piece_copy(i).wait_send()
        for n in range(len(steps)):
            p_copy(n, i).wait_send()
    for u in range(units):
        for n in range(len(steps)):
            c_copy(n, u).wait_send()
    for c in range(nc):
        pair_copy(c).wait_send()
        other_copy(c).wait_send()

    @pl.loop(0, 2)
    def _(f):
        @pl.when(goes_on(f))
        def _():
            @pl.loop(0, nc)
            def _(c):
                for j in range(line):
                    if j < line - 1:
                        @pl.when(j <= place(f))
                        def _(j=j):
                            gather_copy(f, j, c).wait_send()

                    if j:
                        @pl.when(j > place(f))
                        def _(j=j):
                            sum_copy(f, j, c).wait_send()

    for n in range(nc):
        out_copy(lanes(n), n).wait()
        out_copy(sum_lanes(n), nc + n).wait()


def solution(mesh):
    line, cols_n = mesh.shape["row"] // PAIR, mesh.shape["col"]
    n_steps = len(exchanges(cols_n))

    def local(coeffs, ham_alpha, ham_beta):
        rows, cols = coeffs.shape
        half = cols // 2
        cw = min(256, half)
        nc = half // cw
        units = cols // LANES
        f32, dma = jnp.float32, pltpu.SemaphoreType.DMA
        any_spec = pl.BlockSpec(memory_space=pl.ANY)
        return pl.pallas_call(
            functools.partial(kernel, line, cols_n, cw),
            out_shape=jax.ShapeDtypeStruct((rows, cols), f32),
            in_specs=[any_spec, any_spec, any_spec],
            out_specs=any_spec,
            scratch_shapes=[
                pltpu.VMEM((rows, cols), f32),
                pltpu.VMEM((rows, cols), f32),
                pltpu.VMEM((PAIR, line, rows, rows), f32),
                pltpu.VMEM((cols_n, cols, cols), f32),
                pltpu.VMEM((cols_n - 1, rows, cols), f32),
                pltpu.VMEM((2, line - 1, rows, half), f32),
                pltpu.VMEM((2, line, rows, half), f32),
                pltpu.VMEM((PAIR, rows, half), f32),
                pltpu.VMEM((rows, half), f32),
                pltpu.VMEM((PAIR, rows, half), f32),
                dma((2,)),
                dma((line,)),
                dma((cols_n,)),
                dma((2 * nc,)),
                dma((2, line - 1, nc)),
                dma((2, line - 1, nc)),
                dma((2, line, nc)),
                dma((2, line, nc)),
                dma((line,)),
                dma((line,)),
                dma((nc,)),
                dma((nc,)),
                dma((nc,)),
                dma((nc,)),
                dma((n_steps, line)),
                dma((n_steps, line)),
                dma((n_steps, units)),
                dma((n_steps, units)),
            ],
            compiler_params=pltpu.CompilerParams(
                collective_id=0, has_side_effects=True, vmem_limit_bytes=67043328
            ),
        )(coeffs, ham_alpha, ham_beta)

    in_specs = (P("row", "col"), P("row", None), P("col", None))
    return jax.shard_map(
        local, mesh=mesh, in_specs=in_specs, out_specs=P("row", "col"), check_vma=False
    )
```

time: 127 us -> 103 us (0.81)
  Pallas kernels: 124 us -> 99.2 us
    pallas_call x1, Pallas kernels: 124 us -> 99.2 us  [local(): pl.pallas_call(functools.partial(kernel, line, cols_n, cw), out_shape=jax...]
where the time goes in v1:
time: 103 us; the launch traced here: 102 us
  Pallas kernels  99.2 us (96%)
  local copies, waits for them, and re-layouts  3.16 us (3%)
    pallas_call x1, Pallas kernels, local(): pl.pallas_call(functools.partial(kernel, line, cols_n, cw), out_shape=jax...  99.2 us
    unnamed x1, local copies, waits for them, and re-layouts  3.16 us

profile of v1, /device:TPU:0, one launch (start us, length us, event | category | flops | bytes accessed | tf_op | source)
XLA Modules:
  0.0 102.4 jit_solution(3618882818957492949)
XLA Ops:
  0.0 99.2 %shard_map.37 = f32[512,1024]{1,0:T(8,128)} custom-call(f32[512,1024]{1,0:T(8,128)} %coeffs.1, f32[512,4096]{1,0:T(8,128)} %ha.1, f32[1024,4096]{1,0:T(8,128)} %hb.1), custom_call_target="tpu_custom_call" | custom-call | tf_op jit(solution)/shard_map/pallas_call | solution.py:459
  99.2 3.2 %copy.5 = f32[512,1024]{1,0:T(8,128)} copy(f32[512,1024]{1,0:T(8,128)} %shard_map.37) | data formatting | bytes 4194304

commit v2 on v1

--- a/solution.py
+++ b/solution.py
@@ -49,9 +49,9 @@
 
 def kernel(
     line, cols_n, cw,
-    coeffs, ha, hb, result,
-    own, out, ham, beta, co, ag, rs, acc, acc_in, pair,
-    l_sem, h_sem, b_sem, out_sem, a_send, a_recv, r_send, r_recv,
+    coeffs, ha, hb, out,
+    own, ham, beta, co, ag, rs, acc, acc_in, pair,
+    l_sem, h_sem, b_sem, a_send, a_recv, r_send, r_recv,
     x_send, x_recv, k_send, k_recv, o_send, o_recv, p_send, p_recv, c_send, c_recv,
 ):
     rows, cols = coeffs.shape
@@ -380,9 +380,6 @@
         at = sum_lanes(c)
         out[:, at] = out[:, at] + term(z, c)
 
-    def out_copy(at, n):
-        return pltpu.make_async_copy(out.at[:, at], result.at[:, at], out_sem.at[n])
-
     def finish_sums(c):
         at = sum_lanes(c)
 
@@ -393,13 +390,10 @@
                 sum_copy(f, line - 1, c).wait_recv()
                 out[:, at] = out[:, at] + rs[f, line - 1, :, lanes(c)]
 
-        out_copy(at, nc + c).start()
-
     def finish_gathered(c):
         at = lanes(c)
         other_copy(c).wait_recv()
         out[:, at] = out[:, at] + (acc[0, :, at] + acc_in[:, at])
-        out_copy(at, c).start()
 
     @pl.loop(0, nc - 1)
     def _(c):
@@ -439,10 +433,6 @@
                         def _(j=j):
                             sum_copy(f, j, c).wait_send()
 
-    for n in range(nc):
-        out_copy(lanes(n), n).wait()
-        out_copy(sum_lanes(n), nc + n).wait()
-
 
 def solution(mesh):
     line, cols_n = mesh.shape["row"] // PAIR, mesh.shape["col"]
@@ -458,11 +448,10 @@
         any_spec = pl.BlockSpec(memory_space=pl.ANY)
         return pl.pallas_call(
             functools.partial(kernel, line, cols_n, cw),
-            out_shape=jax.ShapeDtypeStruct((rows, cols), f32),
+            out_shape=pltpu.VMEM((rows, cols), f32),
             in_specs=[any_spec, any_spec, any_spec],
-            out_specs=any_spec,
+            out_specs=pl.BlockSpec(memory_space=pltpu.VMEM),
             scratch_shapes=[
-                pltpu.VMEM((rows, cols), f32),
                 pltpu.VMEM((rows, cols), f32),
                 pltpu.VMEM((PAIR, line, rows, rows), f32),
                 pltpu.VMEM((cols_n, cols, cols), f32),
@@ -475,7 +464,6 @@
                 dma((2,)),
                 dma((line,)),
                 dma((cols_n,)),
-                dma((2 * nc,)),
                 dma((2, line - 1, nc)),
                 dma((2, line - 1, nc)),
                 dma((2, line, nc)),
@@ -492,7 +480,7 @@
                 dma((n_steps, units)),
             ],
             compiler_params=pltpu.CompilerParams(
-                collective_id=0, has_side_effects=True, vmem_limit_bytes=67043328
+                collective_id=0, has_side_effects=True, vmem_limit_bytes=58 * 2**20
             ),
         )(coeffs, ham_alpha, ham_beta)
 

time: 103 us -> 99.9 us (0.970)
  local copies, waits for them, and re-layouts: 3.16 us -> 1.32 us
    unnamed x1, local copies, waits for them, and re-layouts: 3.16 us -> 1.32 us
where the time goes in v2:
time: 99.9 us; the launch traced here: 99.8 us
  Pallas kernels  98.4 us (98%)
  local copies, waits for them, and re-layouts  1.32 us (1%)
    pallas_call x1, Pallas kernels, local(): pl.pallas_call(functools.partial(kernel, line, cols_n, cw), out_shape=plt...  98.4 us

profile of v2, /device:TPU:0, one launch (start us, length us, event | category | flops | bytes accessed | tf_op | source)
XLA Modules:
  0.0 99.8 jit_solution(15344648216926274691)
XLA Ops:
  0.0 98.4 %shard_map.37 = f32[512,1024]{1,0:T(8,128)S(1)} custom-call(f32[512,1024]{1,0:T(8,128)} %coeffs.1, f32[512,4096]{1,0:T(8,128)} %ha.1, f32[1024,4096]{1,0:T(8,128)} %hb.1), custom_call_target="tpu_custom_call" | custom-call | tf_op jit(solution)/shard_map/pallas_call | solution.py:449
  98.5 1.3 %copy.5 = f32[512,1024]{1,0:T(8,128)} copy(f32[512,1024]{1,0:T(8,128)S(1)} %shard_map.37) | data formatting | bytes 4194304

commit v3 on v2

--- a/solution.py
+++ b/solution.py
@@ -163,12 +163,22 @@
     def goes_on(f):
         return place(f) < line - 1
 
+    def share(i):
+        return (rows // 2, 2) if isinstance(i, int) and i == 1 else (prow, cols_n)
+
+    def piece_rows(i, index):
+        height, n = share(i)
+        return pl.ds(pl.multiple_of(index % n * height, 8), height)
+
     def piece(i, index):
-        return ham.at[1, slot(i), pl.ds(pl.multiple_of(index * prow, 8), prow)]
+        return ham.at[1, slot(i), piece_rows(i, index)]
+
+    def hops(i):
+        return [[near]] if isinstance(i, int) and i == 1 else groups
 
     def piece_copy(i):
         at = pl.multiple_of((slot(i) * PAIR + 1 - x) * rows, LANES)
-        src = ha.at[pl.ds(pl.multiple_of(col * prow, 8), prow), pl.ds(at, rows)]
+        src = ha.at[piece_rows(i, col), pl.ds(at, rows)]
         return remote(src, piece(i, col), x_send.at[i], x_recv.at[i], (partner, col))
 
     def pair_copy(c):
@@ -224,11 +234,11 @@
 
     def pass_piece(i):
         piece_copy(i).wait_recv()
-        for group in groups:
+        for group in hops(i):
             p_copy(group[0], i).start()
 
     def have_piece(i):
-        for g, group in enumerate(groups):
+        for g, group in enumerate(hops(i)):
             if g:
                 for n in group[1:]:
                     p_copy(n, i).start()
@@ -301,19 +311,14 @@
 
     for j in range(1, line):
         if j == 2:
-            pass_piece(1)
             have_units(0, units // 2)
             for key in range(2, cols_n):
                 add_beta(key, True, 0, cols // 2)
+            pass_piece(1)
             have_piece(1)
 
         @pl.loop(0, nc)
         def _(c, j=j):
-            if j == 2:
-                @pl.when(c + 2 < line)
-                def _():
-                    pass_piece(c + 2)
-
             if j == 1:
                 pair_copy(c).wait_recv()
 
@@ -347,7 +352,16 @@
 
                     sum_copy(f, j, c).start()
 
+            if j == 2:
+                @pl.when(c + 2 < line)
+                def _():
+                    pass_piece(c + 2)
+
             if j == 3:
+                @pl.when(c == 0)
+                def _():
+                    have_piece(line - 1)
+
                 second_products(c)
 
             @pl.loop(0, 2)
@@ -368,7 +382,7 @@
                 pass_piece(i)
             for u in range(units // 2 + 1, units):
                 c_copy(groups[0][0], u).start()
-            for i in range(2, line):
+            for i in range(2, line - 1):
                 have_piece(i)
 
     have_units(units // 2, units)
@@ -403,18 +417,19 @@
     def _(c):
         finish_gathered(c)
 
-    finish_sums(nc - 1)
-
     for i in range(line):
         piece_copy(i).wait_send()
-        for n in range(len(steps)):
-            p_copy(n, i).wait_send()
+        for group in hops(i):
+            for n in group:
+                p_copy(n, i).wait_send()
     for u in range(units):
         for n in range(len(steps)):
             c_copy(n, u).wait_send()
     for c in range(nc):
         pair_copy(c).wait_send()
         other_copy(c).wait_send()
+
+    finish_sums(nc - 1)
 
     @pl.loop(0, 2)
     def _(f):

time: 99.9 us -> 98.5 us (0.986)
  Pallas kernels: 98.4 us -> 97.1 us
    pallas_call x1, Pallas kernels: 98.4 us -> 97.1 us  [local(): pl.pallas_call(functools.partial(kernel, line, cols_n, cw), out_shape=plt...]
where the time goes in v3:
time: 98.5 us; the launch traced here: 98.4 us
  Pallas kernels  97.1 us (99%)
  local copies, waits for them, and re-layouts  1.32 us (1%)
    pallas_call x1, Pallas kernels, local(): pl.pallas_call(functools.partial(kernel, line, cols_n, cw), out_shape=plt...  97.1 us

profile of v3, /device:TPU:0, one launch (start us, length us, event | category | flops | bytes accessed | tf_op | source)
XLA Modules:
  0.0 98.4 jit_solution(2711288670109812756)
XLA Ops:
  0.0 97.1 %shard_map.37 = f32[512,1024]{1,0:T(8,128)S(1)} custom-call(f32[512,1024]{1,0:T(8,128)} %coeffs.1, f32[512,4096]{1,0:T(8,128)} %ha.1, f32[1024,4096]{1,0:T(8,128)} %hb.1), custom_call_target="tpu_custom_call" | custom-call | tf_op jit(solution)/shard_map/pallas_call | solution.py:464
  97.1 1.3 %copy.5 = f32[512,1024]{1,0:T(8,128)} copy(f32[512,1024]{1,0:T(8,128)S(1)} %shard_map.37) | data formatting | bytes 4194304
